TPU v7x, 128 devices: a whole 4x4x4 slice. The times are simulated.
128 devices in a mesh: attn: 8 (over x, core), ffn: 16 (over y, z).
Axes of the slice: x: 4, y: 4, z: 4, core: 2. Of those that a mesh axis runs over, the one named last changes fastest.
Arguments:
- queries: bfloat16 [1024, 2, 64, 576], P(('attn', 'ffn')), may hold values from -9 to 9
- latent_cache: bfloat16 [1024, 512, 576], P(('attn', 'ffn')), may hold values from -4 to 4
- fresh_latent: bfloat16 [1024, 2, 576], P(('attn', 'ffn')), may hold values from -4 to 4
- lengths: int32 [1024], P(('attn', 'ffn')), may hold values from 1 to 512, 262144 in all
- handoff: int32 [16, 8], P('ffn'), may hold values 0 or 1
- residual: bfloat16 [1024, 2, 7168], P(('attn', 'ffn')), may hold values from -30 to 30
- value_up_matrix: bfloat16 [64, 512, 128], P('ffn'), may hold values from -0.5 to 0.5
- output_weight: bfloat16 [8192, 7168], P('ffn'), may hold values from -0.1875 to 0.1875
- norm_gain: float32 [7168], replicated, may hold values from 0.3 to 3
- router: bfloat16 [7168, 16], replicated, may hold values from -0.0625 to 0.0625
- expert_ids: int32 [1024, 2, 2], P('attn'), may hold values from 0 to 15, all different within a row; in each aligned block of 256 rows (0 to 255, 256 to 511, ..., all dimensions but the last counted through in order) at most 64 rows name the same one
- gate_weight: bfloat16 [16, 7168, 2048], P('ffn', None, 'attn'), may hold values from -0.0625 to 0.0625
- up_weight: bfloat16 [16, 7168, 2048], P('ffn', None, 'attn'), may hold values from -0.0625 to 0.0625
- down_weight: bfloat16 [16, 2048, 7168], P('ffn', 'attn'), may hold values from -0.125 to 0.125
Outputs:
- attended: bfloat16 [1024, 2, 7168], P(('attn', 'ffn'))
- expert_out: bfloat16 [1024, 2, 7168], P(('attn', 'ffn'))
Inputs may be any that keep to these rules, and one draw needn't show every extreme that they name: `expert_ids`: the 2 ids of a token differ. In each aligned block of 256 tokens (the requests of one index of attn, all new tokens of each, in order) no expert is chosen by more than 64 tokens, and some expert is chosen by exactly 64 in some block.
All inputs are finite; a program needn't handle non-finite values. No bound on the sum of `lengths` or of `handoff` on one device may be relied on, other than what follows from the above.
Results may differ from a plain program's by a relative error of at most 0.014.
Values may be sent and summed in bfloat16 or wider, within the bound.
A program may use at most 128 MiB of HBM per device.

v0:
```python
import jax
import jax.numpy as jnp
from jax import lax
from jax.sharding import PartitionSpec as P

KV_RANK = 512
score_scale = 192.0 ** (-0.5)
norm_epsilon = 1e-06


def shifted(value, axis, by):
    count = lax.axis_size(axis)
    return lax.ppermute(value, axis, [(i, (i + by) % count) for i in range(count)])


def attend_block(queries, latent_cache, fresh_latent, lengths):
    req_count, steps_here, heads_here, latent_width = queries.shape
    cache_span = latent_cache.shape[1]
    row_count = steps_here * heads_here
    rows_flat = queries.reshape(req_count, row_count, latent_width)
    old_scores = (
        jnp.einsum("rqc,rnc->rqn", rows_flat, latent_cache, preferred_element_type=jnp.float32)
        * score_scale
    )
    position = lax.broadcasted_iota(jnp.int32, (1, 1, cache_span), 2)
    old_scores = jnp.where(position < lengths[:, None, None], old_scores, -jnp.inf)
    new_scores = (
        jnp.einsum("rqc,rjc->rqj", rows_flat, fresh_latent, preferred_element_type=jnp.float32)
        * score_scale
    )
    row_step = lax.broadcasted_iota(jnp.int32, (1, row_count, steps_here), 1) // heads_here
    column_step = lax.broadcasted_iota(jnp.int32, (1, row_count, steps_here), 2)
    new_scores = jnp.where(column_step <= row_step, new_scores, -jnp.inf)
    row_peak = jnp.maximum(jnp.max(old_scores, axis=2), jnp.max(new_scores, axis=2))[:, :, None]
    old_exp = jnp.exp(old_scores - row_peak)
    new_exp = jnp.exp(new_scores - row_peak)
    denominator = jnp.sum(old_exp, axis=2, keepdims=True) + jnp.sum(new_exp, axis=2, keepdims=True)
    old_probs = (old_exp / denominator).astype(jnp.bfloat16)
    new_probs = (new_exp / denominator).astype(jnp.bfloat16)
    latent_mix = jnp.einsum(
        "rqn,rnc->rqc", old_probs, latent_cache[:, :, :KV_RANK], preferred_element_type=jnp.float32
    )
    latent_mix = latent_mix + jnp.einsum(
        "rqj,rjc->rqc", new_probs, fresh_latent[:, :, :KV_RANK], preferred_element_type=jnp.float32
    )
    return latent_mix.astype(jnp.bfloat16).reshape(req_count, steps_here, heads_here, KV_RANK)


def rms_normalize(state, norm_gain):
    scale_rows = lax.rsqrt(jnp.mean(state * state, axis=-1, keepdims=True) + norm_epsilon)
    return (state * scale_rows * norm_gain).astype(jnp.bfloat16)


def local(
    queries,
    latent_cache,
    fresh_latent,
    lengths,
    handoff,
    residual,
    value_up_matrix,
    output_weight,
    norm_gain,
    router,
    expert_ids,
    gate_weight,
    up_weight,
    down_weight,
):
    moved_flag = handoff[0] == 1
    moved_here = moved_flag[:, None, None, None]
    arrived = shifted((queries, latent_cache, fresh_latent, lengths), "attn", 1)
    queries_now = jnp.where(moved_here, arrived[0], queries)
    cache_now = jnp.where(moved_here[:, :, :, 0], arrived[1], latent_cache)
    fresh_now = jnp.where(moved_here[:, :, :, 0], arrived[2], fresh_latent)
    lengths_now = jnp.where(moved_flag, arrived[3], lengths)
    latent_out = attend_block(queries_now, cache_now, fresh_now, lengths_now)
    heads_local = value_up_matrix.shape[0]
    model_width = output_weight.shape[1]
    head_weight = output_weight.reshape(heads_local, value_up_matrix.shape[2], model_width)
    value_rows = jnp.einsum(
        "olfb,fbw->olfw",
        lax.all_to_all(latent_out, "ffn", split_axis=2, concat_axis=0, tiled=True),
        value_up_matrix,
        preferred_element_type=jnp.float32,
    ).astype(jnp.bfloat16)
    partial_out = jnp.einsum(
        "rshv,hvd->rsd", value_rows, head_weight, preferred_element_type=jnp.float32
    )
    req_dev = residual.shape[0]
    steps_here = residual.shape[1]
    ffn_index = lax.axis_index("ffn")
    local_token_rows = residual.astype(jnp.float32)
    placed_rows = lax.dynamic_update_slice(
        jnp.zeros_like(partial_out), local_token_rows, (ffn_index * req_dev, 0, 0)
    )
    state_rows = lax.psum(partial_out + placed_rows, "ffn")
    own_state = lax.dynamic_slice_in_dim(state_rows, ffn_index * req_dev, req_dev, 0)
    normed_rows = rms_normalize(state_rows, norm_gain)
    attended = own_state.astype(jnp.bfloat16)
    row_req = normed_rows.shape[0]
    row_tokens = row_req * steps_here
    normed_flat = normed_rows.reshape(row_tokens, model_width)
    expert_count = router.shape[1]
    logits = jnp.dot(normed_flat, router, preferred_element_type=jnp.float32)
    affinity = jax.nn.sigmoid(logits)
    ids_flat = expert_ids.reshape(row_tokens, expert_ids.shape[2])
    onehot = ids_flat[:, :, None] == lax.broadcasted_iota(jnp.int32, (1, 1, expert_count), 2)
    chosen = jnp.sum(jnp.where(onehot, affinity[:, None, :], 0.0), axis=2)
    gate_fraction_value = 2.5 * chosen / jnp.sum(chosen, axis=1, keepdims=True)
    routed_here = ids_flat == ffn_index
    token_weight = jnp.sum(jnp.where(routed_here, gate_fraction_value, 0.0), axis=1)
    token_hit = jnp.sum(routed_here.astype(jnp.int32), axis=1)
    slot_rank = jnp.cumsum(token_hit) - 1
    capacity = 4 * steps_here * req_dev
    slot_ids = lax.broadcasted_iota(jnp.int32, (capacity, row_tokens), 0)
    selector = ((token_hit[None, :] == 1) & (slot_rank[None, :] == slot_ids)).astype(jnp.bfloat16)
    expert_input = jnp.dot(selector, normed_flat, preferred_element_type=jnp.float32).astype(
        jnp.bfloat16
    )
    gate_local = gate_weight[0]
    up_local = up_weight[0]
    down_local = down_weight[0]
    rows_in = lax.all_gather(expert_input, "attn", axis=0, tiled=True)
    gate_part = jnp.dot(rows_in, gate_local, preferred_element_type=jnp.float32)
    up_part = jnp.dot(rows_in, up_local, preferred_element_type=jnp.float32)
    hidden_all = (jax.nn.silu(gate_part) * up_part).astype(jnp.bfloat16)
    rows_in = hidden_all
    expert_rows = lax.psum_scatter(
        jnp.dot(rows_in, down_local, preferred_element_type=jnp.float32),
        "attn",
        scatter_dimension=0,
        tiled=True,
    ).astype(jnp.bfloat16)
    returned = (
        jnp.einsum("ct,cd->td", selector, expert_rows, preferred_element_type=jnp.float32)
        * token_weight[:, None]
    )
    summed = lax.psum_scatter(
        returned.reshape(row_req, steps_here, model_width), "ffn", scatter_dimension=0, tiled=True
    )
    return (attended, summed.astype(jnp.bfloat16))


def solution(mesh):
    return jax.shard_map(
        local,
        mesh=mesh,
        in_specs=(
            P(("attn", "ffn"), None, None, None),
            P(("attn", "ffn"), None, None),
            P(("attn", "ffn"), None, None),
            P(("attn", "ffn")),
            P("ffn", None),
            P(("attn", "ffn"), None, None),
            P("ffn", None, None),
            P("ffn", None),
            P(),
            P(),
            P("attn", None, None),
            P("ffn", None, "attn"),
            P("ffn", None, "attn"),
            P("ffn", "attn", None),
        ),
        out_specs=(P(("attn", "ffn"), None, None), P(("attn", "ffn"), None, None)),
        check_vma=False,
    )
```

profile of v0, /device:TPU:0, one launch (start us, length us, event | category | flops | bytes accessed | tf_op | source)
XLA Modules:
  0.0 625.4 jit_solution(17319362532799770855)
XLA Ops:
  7.2 1.7 collective-permute-start.3
  9.0 1.6 collective-permute-start
  10.5 7.7 %copy.103 = bf16[8,512,576]{2,1,0:T(8,128)(2,1)} copy(bf16[8,512,576]{1,2,0:T(8,128)(2,1)} %param.15) | data formatting | bytes 9437184 | tf_op args[1]
  18.3 58.3 %collective-permute-done = s32[8]{0:T(128)S(1)} collective-permute-done((s32[8]{0:T(128)}, s32[8]{0:T(128)S(1)}, u32[]{:S(2)}, u32[]{:S(2)}) %collective-permute-start) | collective-permute-done | bytes 64 | tf_op jit(solution)/shard_map/ppermute | solution.py:13
  76.8 1.5 broadcast_select_fusion.1
  78.3 0.5 fusion.60
  78.8 7.7 %copy.102 = bf16[8,512,576]{2,1,0:T(8,128)(2,1)} copy(bf16[8,512,576]{1,2,0:T(8,128)(2,1)} %collective-permute-done.2) | data formatting | bytes 9437184 | tf_op jit(solution)/shard_map/ppermute | solution.py:13
  86.6 4.7 broadcast_select_fusion
  91.2 1.9 fusion.8
  93.1 0.6 fusion.11
  93.8 0.5 fusion.50
  94.3 1.3 add_convert_fusion
  95.6 1.6 copy.107
  97.2 8.1 %all-to-all-start = ((bf16[8,2,64,512]{3,0,1,2:T(8,128)(2,1)}), bf16[8,2,64,512]{3,0,1,2:T(8,128)(2,1)S(1)}, u32[]{:S(2)}, u32[]{:S(2)}) async-start(bf16[8,2,64,512]{3,0,1,2:T(8,128)(2,1)} %copy.107), calls=%async_computation | async-start | bytes 2097152 | tf_op jit(solution)/shard_map/all_to_all | solution.py:83
  105.4 15.1 %all-to-all-done = bf16[8,2,64,512]{3,0,1,2:T(8,128)(2,1)S(1)} async-done(((bf16[8,2,64,512]{3,0,1,2:T(8,128)(2,1)}), bf16[8,2,64,512]{3,0,1,2:T(8,128)(2,1)S(1)}, u32[]{:S(2)}, u32[]{:S(2)}) %all-to-all-start) | async-done | bytes 1048608 | tf_op jit(solution)/shard_map/all_to_all | solution.py:83
  120.5 6.7 %convolution_bitcast_fusion = f32[128,2,7168]{2,0,1:T(8,128)} fusion(bf16[4,128,7168,1]{2,1,0,3:T(8,128)(2,1)} %bitcast.61, bf16[16,8,2,4,512]{4,1,2,3,0:T(8,128)(2,1)S(1)} %bitcast.62, bf16[4,512,128]{2,1,0:T(8,128)(2,1)S(1)} %copy-done), kind=kOutput, calls=%fused_computation.1 | convolution fusion | flops 2013396992 | bytes 16252928 | tf_op jit(solution)/shard_map/rshv,hvd->rsd/dot_general | solution.py:87
  127.2 1.9 add_dynamic-update-slice_fusion
  129.1 0.2 all-gather.2.cloned.1.call-start
  129.3 0.4 copy-done.8
  129.9 0.1 reshape.167
  130.0 0.3 reduce-window.9
  130.4 0.1 copy.111
  130.6 0.2 eq.65
  130.9 127.7 %all-reduce.4.cloned.1.call-done = f32[128,2,7168]{2,0,1:T(8,128)} async-done(((f32[128,2,7168]{2,0,1:T(8,128)}), f32[128,2,7168]{2,0,1:T(8,128)}) %all-reduce.4.cloned.1.call-update) | async-done | bytes 7340048 | tf_op jit(solution)/shard_map/psum | solution.py:97
  258.7 3.8 multiply_reduce_fusion
  262.5 1.3 copy-done.2
  263.8 1.0 multiply_convert_fusion
  264.8 5.6 copy.113
  270.4 8.4 %reshape.169 = bf16[256,7168]{1,0:T(8,128)(2,1)} reshape(bf16[128,2,7168]{2,1,0:T(2,128)(2,1)} %copy.113) | data formatting | bytes 7340032 | tf_op jit(solution)/shard_map/reshape | solution.py:103
  278.8 3.7 convolution_convert_fusion
  282.6 0.3 reduce-scatter.2.cloned.1.call-start
  282.8 44.9 %all-gather.2.cloned.1.call-done = bf16[512,7168]{1,0:T(8,128)(2,1)} async-done(((bf16[64,7168]{1,0:T(8,128)(2,1)}), bf16[512,7168]{1,0:T(8,128)(2,1)}) %all-gather.2.cloned.1.call-update) | async-done | bytes 7340048 | tf_op jit(solution)/shard_map/all_gather | solution.py:124
  327.7 6.2 fusion.6
  333.9 18.2 %fusion.2 = f32[512,7168]{1,0:T(8,128)} fusion(bf16[1,256,7168]{2,1,0:T(8,128)(2,1)} %param.27, bf16[512,7168]{1,0:T(8,128)(2,1)} %all-gather.2.cloned.1.call-done, bf16[1,7168,256]{2,1,0:T(8,128)(2,1)} %param.26, f32[512,256]{1,0:T(8,128)S(1)} %fusion.6), kind=kOutput, calls=%fused_computation.8 | convolution fusion | flops 3758882816 | bytes 29884416 | tf_op jit(solution)/shard_map/dot_general | solution.py:130
  352.3 0.1 eq.68
  352.4 0.3 copy-done.11
  352.8 0.6 dynamic-slice.1
  354.0 1.1 dynamic-slice_convert_fusion.1
  355.1 0.9 copy.118
  356.0 3.1 fusion.21
  359.1 0.1 mul.76
  359.4 0.1 div.59
  359.7 0.1 mul.77
  359.9 74.9 %reduce-scatter.2.cloned.1.call-done = f32[64,7168]{1,0:T(8,128)} async-done(((f32[512,7168]{1,0:T(8,128)}), f32[64,7168]{1,0:T(8,128)}) %reduce-scatter.2.cloned.1.call-update) | async-done | bytes 1835024 | tf_op jit(solution)/shard_map/reduce_scatter | solution.py:129
  434.8 5.6 convolution_multiply_fusion
  440.4 9.3 %reshape.170 = f32[128,2,7168]{2,1,0:T(2,128)} reshape(f32[256,7168]{1,0:T(8,128)} %convolution_multiply_fusion) | data formatting | bytes 14680064 | tf_op jit(solution)/shard_map/reshape | solution.py:140
  449.8 167.4 %all-reduce.5 = bf16[128,2,7168]{2,1,0:T(2,128)(2,1)} all-reduce(f32[128,2,7168]{2,1,0:T(2,128)} %reshape.170), channel_id=3, replica_groups=mesh['attn'=8,'ffn'=16] {'ffn'}, use_global_device_ids=true, to_apply=%region_13.14.clone | all-reduce | flops 1835008 | bytes 11010048
  617.1 1.8 dynamic-slice_convert_fusion
  (55 shorter events, 1.3 us)
Async XLA Ops:
  7.2 113.4 %copy-start = (bf16[4,512,128]{2,1,0:T(8,128)(2,1)S(1)}, bf16[4,512,128]{2,1,0:T(8,128)(2,1)}, u32[]{:S(2)}) copy-start(bf16[4,512,128]{2,1,0:T(8,128)(2,1)} %param.20) | copy-start | bytes 1572868
  7.2 69.5 %copy-start.7 = (bf16[8,2,576]{2,1,0:T(2,128)(2,1)S(1)}, bf16[8,2,576]{2,1,0:T(2,128)(2,1)}, u32[]{:S(2)}) copy-start(bf16[8,2,576]{2,1,0:T(2,128)(2,1)} %param.16) | copy-start | bytes 55300
  7.2 69.6 %copy-start.3 = (bf16[8,2,64,576]{3,2,1,0:T(8,128)(2,1)S(1)}, bf16[8,2,64,576]{3,2,1,0:T(8,128)(2,1)}, u32[]{:S(2)}) copy-start(bf16[8,2,64,576]{3,2,1,0:T(8,128)(2,1)} %param.14) | copy-start | bytes 3538948
  7.2 69.4 %copy-start.10 = (s32[8]{0:T(128)S(1)}, s32[8]{0:T(128)}, u32[]{:S(2)}) copy-start(s32[8]{0:T(128)} %param.17) | copy-start | bytes 100
  7.2 11.0 %copy-start.9 = (s32[1,8]{1,0:T(1,128)S(1)}, s32[1,8]{1,0:T(1,128)}, u32[]{:S(2)}) copy-start(s32[1,8]{1,0:T(1,128)} %param.18) | copy-start | bytes 100
  7.2 71.6 %collective-permute-start.2 = (bf16[8,512,576]{1,2,0:T(8,128)(2,1)}, bf16[8,512,576]{1,2,0:T(8,128)(2,1)}, u32[]{:S(2)}, u32[]{:S(2)}) collective-permute-start(bf16[8,512,576]{1,2,0:T(8,128)(2,1)} %param.15), channel_id=1, source_target_pairs={{0,16},{16,32},{32,48},{48,64},{64,80},{80,96},{96,112},{112,0},{1... | collective-permute-start | bytes 14155784 | tf_op jit(solution)/shard_map/ppermute | solution.py:13
  7.2 69.4 %collective-permute-start.3 = (bf16[8,2,576]{2,1,0:T(2,128)(2,1)}, bf16[8,2,576]{2,1,0:T(2,128)(2,1)S(1)}, u32[]{:S(2)}, u32[]{:S(2)}) collective-permute-start(bf16[8,2,576]{2,1,0:T(2,128)(2,1)} %param.16), channel_id=1, source_target_pairs={{0,16},{16,32},{32,48},{48,64},{64,80},{80,96},{96,112},{112,0},{1... | collective-permute-start | bytes 55304 | tf_op jit(solution)/shard_map/ppermute | solution.py:13
  8.9 67.8 %collective-permute-start.1 = (bf16[8,2,64,576]{3,2,1,0:T(8,128)(2,1)}, bf16[8,2,64,576]{3,2,1,0:T(8,128)(2,1)}, u32[]{:S(2)}, u32[]{:S(2)}) collective-permute-start(bf16[8,2,64,576]{3,2,1,0:T(8,128)(2,1)} %param.14), channel_id=1, source_target_pairs={{0,16},{16,32},{32,48},{48,64},{64,80},{80,96},{96,112},{112,0},{1... | collective-permute-start | bytes 3538952 | tf_op jit(solution)/shard_map/ppermute | solution.py:13
  9.0 67.6 %collective-permute-start = (s32[8]{0:T(128)}, s32[8]{0:T(128)S(1)}, u32[]{:S(2)}, u32[]{:S(2)}) collective-permute-start(s32[8]{0:T(128)} %param.17), channel_id=1, source_target_pairs={{0,16},{16,32},{32,48},{48,64},{64,80},{80,96},{96,112},{112,0},{1... | collective-permute-start | bytes 104 | tf_op jit(solution)/shard_map/ppermute | solution.py:13
  97.2 23.3 %all-to-all-start = ((bf16[8,2,64,512]{3,0,1,2:T(8,128)(2,1)}), bf16[8,2,64,512]{3,0,1,2:T(8,128)(2,1)S(1)}, u32[]{:S(2)}, u32[]{:S(2)}) async-start(bf16[8,2,64,512]{3,0,1,2:T(8,128)(2,1)} %copy.107), calls=%async_computation | async-start | bytes 2097152 | tf_op jit(solution)/shard_map/all_to_all | solution.py:83
  105.3 153.3 %all-reduce.4.cloned.1.call-start = ((), (), s32[]{:S(2)}) async-start(), calls=%async_computation.2 | async-start | bytes 14680064 | tf_op jit(solution)/shard_map/psum | solution.py:97
  120.5 6.7 %copy-start.4 = (bf16[8,2,7168]{2,1,0:T(2,128)(2,1)S(1)}, bf16[8,2,7168]{2,1,0:T(2,128)(2,1)}, u32[]{:S(2)}) copy-start(bf16[8,2,7168]{2,1,0:T(2,128)(2,1)} %param.19) | copy-start | bytes 688132
  129.1 0.7 copy-start.8
  129.1 133.4 %copy-start.6 = (f32[7168]{0:T(1024)S(1)}, f32[7168]{0:T(1024)}, u32[]{:S(2)}) copy-start(f32[7168]{0:T(1024)} %param.22) | copy-start | bytes 86020
  129.1 198.6 %all-gather.2.cloned.1.call-start = ((), (), s32[]{:S(2)}) async-start(), calls=%async_computation.3 | async-start | bytes 8257536 | tf_op jit(solution)/shard_map/all_gather | solution.py:124
  258.7 5.2 copy-start.2
  282.6 152.2 %reduce-scatter.2.cloned.1.call-start = ((), (), s32[]{:S(2)}) async-start(), calls=%async_computation.4 | async-start | bytes 16515072 | tf_op jit(solution)/shard_map/reduce_scatter | solution.py:129
  352.1 0.7 copy-start.11
  352.1 3.9 copy-start.5
  440.4 178.5 %copy-start.1 = (bf16[4,512,128]{2,1,0:T(8,128)(2,1)S(1)}, bf16[4,512,128]{2,1,0:T(8,128)(2,1)}, u32[]{:S(2)}) copy-start(bf16[4,512,128]{2,1,0:T(8,128)(2,1)} %param.20) | copy-start | bytes 1572868
Sparse Core Ops, SparseCore 0:
  129.2 129.4 all-reduce.3
  282.7 44.9 all-gather.1
  352.3 82.5 reduce-scatter.1
where the time goes:
time: 627 us; the launch traced here: 625 us
  waiting for transfers between devices  321 us (51%)
  blocking collectives  167 us (27%)
  local copies, waits for them, and re-layouts  48.5 us (8%)
  matrix products  47.7 us (8%)
  between operations  14.7 us (2%)
  other arithmetic  14.2 us (2%)
  starting transfers between devices  12 us (2%)
    unnamed x1, blocking collectives  167 us
    psum x1, waiting for transfers between devices, local(): state_rows = lax.psum(partial_out + placed_rows, 'ffn')  128 us
    reduce_scatter x1, waiting for transfers between devices, local(): lax.psum_scatter(jnp.dot(rows_in, down_local, preferred_element_type=jnp....  74.9 us
    ppermute x4, waiting for transfers between devices, shifted(): lax.ppermute(value, axis, [(i, (i + by) % count) for i in range(count)])  58.3 us
    all_gather x1, waiting for transfers between devices, local(): rows_in = lax.all_gather(expert_input, 'attn', axis=0, tiled=True)  44.9 us
    dot_general x1, matrix products, local(): jnp.dot(rows_in, down_local, preferred_element_type=jnp.float32)  18.2 us
    all_to_all x1, waiting for transfers between devices, local(): lax.all_to_all(latent_out, 'ffn', split_axis=2, concat_axis=0, tiled=True)  15.1 us
  transfers between devices with their start and end apart: 8, of which 5 were waited for; matrix products, arithmetic and copies ran while one was open for 3% of the time, Pallas kernels for 0%

commit v1 on v0

--- a/solution.py
+++ b/solution.py
@@ -6,6 +6,12 @@
 KV_RANK = 512
 score_scale = 192.0 ** (-0.5)
 norm_epsilon = 1e-06
+
+
+def stacked_exchange(x, name, split, join):
+    pieces = jnp.split(x, lax.axis_size(name), axis=split)
+    got = lax.all_to_all(jnp.stack(pieces), name, 0, 0)
+    return jnp.concatenate(got, axis=join)
 
 
 def shifted(value, axis, by):
@@ -80,7 +86,7 @@
     head_weight = output_weight.reshape(heads_local, value_up_matrix.shape[2], model_width)
     value_rows = jnp.einsum(
         "olfb,fbw->olfw",
-        lax.all_to_all(latent_out, "ffn", split_axis=2, concat_axis=0, tiled=True),
+        stacked_exchange(latent_out, "ffn", 2, 0),
         value_up_matrix,
         preferred_element_type=jnp.float32,
     ).astype(jnp.bfloat16)

time: 627 us -> 636 us (1.014)
  local copies, waits for them, and re-layouts: 48.5 us -> 57.3 us
    unnamed x28 -> x43, local copies, waits for them, and re-layouts: 11.5 us -> 21.2 us
where the time goes in v1:
time: 636 us; the launch traced here: 635 us
  waiting for transfers between devices  321 us (50%)
  blocking collectives  167 us (26%)
  local copies, waits for them, and re-layouts  57.3 us (9%)
  matrix products  48.4 us (8%)
  between operations  14.7 us (2%)
  other arithmetic  14.2 us (2%)
  starting transfers between devices  12 us (2%)
    unnamed x1, blocking collectives  167 us
    psum x1, waiting for transfers between devices, local(): state_rows = lax.psum(partial_out + placed_rows, 'ffn')  128 us
    reduce_scatter x1, waiting for transfers between devices, local(): lax.psum_scatter(jnp.dot(rows_in, down_local, preferred_element_type=jnp....  74.9 us
    ppermute x4, waiting for transfers between devices, shifted(): lax.ppermute(value, axis, [(i, (i + by) % count) for i in range(count)])  58.3 us
    all_gather x1, waiting for transfers between devices, local(): rows_in = lax.all_gather(expert_input, 'attn', axis=0, tiled=True)  44.9 us
    unnamed x43, local copies, waits for them, and re-layouts  21.2 us
    dot_general x1, matrix products, local(): jnp.dot(rows_in, down_local, preferred_element_type=jnp.float32)  18.2 us
    all_to_all x1, waiting for transfers between devices, stacked_exchange(): got = lax.all_to_all(jnp.stack(pieces), name, 0, 0)  15.1 us
  transfers between devices with their start and end apart: 8, of which 5 were waited for; matrix products, arithmetic and copies ran while one was open for 3% of the time, Pallas kernels for 0%

profile of v1, /device:TPU:0, one launch (start us, length us, event | category | flops | bytes accessed | tf_op | source)
XLA Modules:
  0.0 634.9 jit_solution(3954611770264681464)
XLA Ops:
  7.2 1.7 collective-permute-start.3
  9.0 1.6 collective-permute-start
  10.5 7.7 %copy.82 = bf16[8,512,576]{2,1,0:T(8,128)(2,1)} copy(bf16[8,512,576]{1,2,0:T(8,128)(2,1)} %param.15) | data formatting | bytes 9437184 | tf_op args[1]
  18.3 58.3 %collective-permute-done = s32[8]{0:T(128)S(1)} collective-permute-done((s32[8]{0:T(128)}, s32[8]{0:T(128)S(1)}, u32[]{:S(2)}, u32[]{:S(2)}) %collective-permute-start) | collective-permute-done | bytes 64 | tf_op jit(solution)/shard_map/ppermute | solution.py:19
  76.8 1.5 broadcast_select_fusion.1
  78.8 7.7 %copy.81 = bf16[8,512,576]{2,1,0:T(8,128)(2,1)} copy(bf16[8,512,576]{1,2,0:T(8,128)(2,1)} %collective-permute-done.2) | data formatting | bytes 9437184 | tf_op jit(solution)/shard_map/ppermute | solution.py:19
  86.6 4.7 broadcast_select_fusion
  91.2 1.9 fusion.8
  93.1 0.6 fusion.11
  94.3 1.3 add_convert_fusion
  95.6 0.6 fusion.58
  96.3 0.7 fusion.57
  96.9 0.6 fusion.56
  97.6 0.7 fusion.55
  98.2 0.6 fusion.54
  98.8 0.7 fusion.53
  99.5 0.6 fusion.52
  100.1 0.7 fusion.51
  100.8 0.6 fusion.50
  101.4 0.7 fusion.49
  102.1 0.6 fusion.48
  102.7 0.7 fusion.47
  103.4 0.6 fusion.46
  104.0 0.7 fusion.45
  104.7 0.6 fusion.44
  105.3 0.7 fusion.43
  106.0 8.1 %all-to-all-start = ((bf16[16,8,2,4,512]{4,3,2,1,0:T(4,128)(2,1)}), bf16[16,8,2,4,512]{4,3,2,1,0:T(4,128)(2,1)S(1)}, u32[]{:S(2)}, u32[]{:S(2)}) async-start(bf16[16,8,2,4,512]{4,3,2,1,0:T(4,128)(2,1)} %fusion.43), calls=%async_computation | async-start | bytes 2097152 | tf_op jit(solution)/shard_map/all_to_all | solution.py:13
  114.2 15.1 %all-to-all-done = bf16[16,8,2,4,512]{4,3,2,1,0:T(4,128)(2,1)S(1)} async-done(((bf16[16,8,2,4,512]{4,3,2,1,0:T(4,128)(2,1)}), bf16[16,8,2,4,512]{4,3,2,1,0:T(4,128)(2,1)S(1)}, u32[]{:S(2)}, u32[]{:S(2)}) %all-to-all-start) | async-done | bytes 1048608 | tf_op jit(solution)/shard_map/all_to_all | solution.py:13
  129.3 7.3 %convolution_bitcast_fusion = f32[128,2,7168]{2,0,1:T(8,128)} fusion(bf16[4,128,7168,1]{2,1,0,3:T(8,128)(2,1)} %bitcast.122, bf16[16,8,2,4,512]{4,3,2,1,0:T(4,128)(2,1)S(1)} %all-to-all-done, bf16[4,512,128]{2,1,0:T(8,128)(2,1)S(1)} %copy-done), kind=kOutput, calls=%fused_computation.1 | convolution fusion | flops 2013396992 | bytes 16252928 | tf_op jit(solution)/shard_map/rshv,hvd->rsd/dot_general | solution.py:93
  136.7 1.9 add_dynamic-update-slice_fusion
  140.4 127.7 %all-reduce.4.cloned.1.call-done = f32[128,2,7168]{2,0,1:T(8,128)} async-done(((f32[128,2,7168]{2,0,1:T(8,128)}), f32[128,2,7168]{2,0,1:T(8,128)}) %all-reduce.4.cloned.1.call-update) | async-done | bytes 7340048 | tf_op jit(solution)/shard_map/psum | solution.py:103
  268.1 3.8 multiply_reduce_fusion
  272.0 1.3 copy-done.2
  273.3 1.0 multiply_convert_fusion
  274.3 5.6 copy.90
  279.9 8.4 %reshape.173 = bf16[256,7168]{1,0:T(8,128)(2,1)} reshape(bf16[128,2,7168]{2,1,0:T(2,128)(2,1)} %copy.90) | data formatting | bytes 7340032 | tf_op jit(solution)/shard_map/reshape | solution.py:109
  288.3 3.7 convolution_convert_fusion
  292.3 44.9 %all-gather.2.cloned.1.call-done = bf16[512,7168]{1,0:T(8,128)(2,1)} async-done(((bf16[64,7168]{1,0:T(8,128)(2,1)}), bf16[512,7168]{1,0:T(8,128)(2,1)}) %all-gather.2.cloned.1.call-update) | async-done | bytes 7340048 | tf_op jit(solution)/shard_map/all_gather | solution.py:130
  337.2 6.2 fusion.6
  343.4 18.2 %fusion.2 = f32[512,7168]{1,0:T(8,128)} fusion(bf16[1,256,7168]{2,1,0:T(8,128)(2,1)} %param.27, bf16[512,7168]{1,0:T(8,128)(2,1)} %all-gather.2.cloned.1.call-done, bf16[1,7168,256]{2,1,0:T(8,128)(2,1)} %param.26, f32[512,256]{1,0:T(8,128)S(1)} %fusion.6), kind=kOutput, calls=%fused_computation.8 | convolution fusion | flops 3758882816 | bytes 29884416 | tf_op jit(solution)/shard_map/dot_general | solution.py:136
  363.5 1.1 dynamic-slice_convert_fusion.1
  364.5 0.9 copy.95
  365.5 3.1 fusion.21
  369.3 74.9 %reduce-scatter.2.cloned.1.call-done = f32[64,7168]{1,0:T(8,128)} async-done(((f32[512,7168]{1,0:T(8,128)}), f32[64,7168]{1,0:T(8,128)}) %reduce-scatter.2.cloned.1.call-update) | async-done | bytes 1835024 | tf_op jit(solution)/shard_map/reduce_scatter | solution.py:135
  444.3 5.6 convolution_multiply_fusion
  449.9 9.3 %reshape.174 = f32[128,2,7168]{2,1,0:T(2,128)} reshape(f32[256,7168]{1,0:T(8,128)} %convolution_multiply_fusion) | data formatting | bytes 14680064 | tf_op jit(solution)/shard_map/reshape | solution.py:146
  459.2 167.4 %all-reduce.5 = bf16[128,2,7168]{2,1,0:T(2,128)(2,1)} all-reduce(f32[128,2,7168]{2,1,0:T(2,128)} %reshape.174), channel_id=3, replica_groups=mesh['attn'=8,'ffn'=16] {'ffn'}, use_global_device_ids=true, to_apply=%region_13.14.clone | all-reduce | flops 1835008 | bytes 11010048
  626.6 1.8 dynamic-slice_convert_fusion
  (70 shorter events, 5.5 us)
Async XLA Ops:
  7.2 122.2 %copy-start = (bf16[4,512,128]{2,1,0:T(8,128)(2,1)S(1)}, bf16[4,512,128]{2,1,0:T(8,128)(2,1)}, u32[]{:S(2)}) copy-start(bf16[4,512,128]{2,1,0:T(8,128)(2,1)} %param.20) | copy-start | bytes 1572868
  7.2 69.5 %copy-start.7 = (bf16[8,2,576]{2,1,0:T(2,128)(2,1)S(1)}, bf16[8,2,576]{2,1,0:T(2,128)(2,1)}, u32[]{:S(2)}) copy-start(bf16[8,2,576]{2,1,0:T(2,128)(2,1)} %param.16) | copy-start | bytes 55300
  7.2 69.6 %copy-start.3 = (bf16[8,2,64,576]{3,2,1,0:T(8,128)(2,1)S(1)}, bf16[8,2,64,576]{3,2,1,0:T(8,128)(2,1)}, u32[]{:S(2)}) copy-start(bf16[8,2,64,576]{3,2,1,0:T(8,128)(2,1)} %param.14) | copy-start | bytes 3538948
  7.2 69.4 %copy-start.10 = (s32[8]{0:T(128)S(1)}, s32[8]{0:T(128)}, u32[]{:S(2)}) copy-start(s32[8]{0:T(128)} %param.17) | copy-start | bytes 100
  7.2 11.0 %copy-start.9 = (s32[1,8]{1,0:T(1,128)S(1)}, s32[1,8]{1,0:T(1,128)}, u32[]{:S(2)}) copy-start(s32[1,8]{1,0:T(1,128)} %param.18) | copy-start | bytes 100
  7.2 71.6 %collective-permute-start.2 = (bf16[8,512,576]{1,2,0:T(8,128)(2,1)}, bf16[8,512,576]{1,2,0:T(8,128)(2,1)}, u32[]{:S(2)}, u32[]{:S(2)}) collective-permute-start(bf16[8,512,576]{1,2,0:T(8,128)(2,1)} %param.15), channel_id=1, source_target_pairs={{0,16},{16,32},{32,48},{48,64},{64,80},{80,96},{96,112},{112,0},{1... | collective-permute-start | bytes 14155784 | tf_op jit(solution)/shard_map/ppermute | solution.py:19
  7.2 69.4 %collective-permute-start.3 = (bf16[8,2,576]{2,1,0:T(2,128)(2,1)}, bf16[8,2,576]{2,1,0:T(2,128)(2,1)S(1)}, u32[]{:S(2)}, u32[]{:S(2)}) collective-permute-start(bf16[8,2,576]{2,1,0:T(2,128)(2,1)} %param.16), channel_id=1, source_target_pairs={{0,16},{16,32},{32,48},{48,64},{64,80},{80,96},{96,112},{112,0},{1... | collective-permute-start | bytes 55304 | tf_op jit(solution)/shard_map/ppermute | solution.py:19
  8.9 67.8 %collective-permute-start.1 = (bf16[8,2,64,576]{3,2,1,0:T(8,128)(2,1)}, bf16[8,2,64,576]{3,2,1,0:T(8,128)(2,1)}, u32[]{:S(2)}, u32[]{:S(2)}) collective-permute-start(bf16[8,2,64,576]{3,2,1,0:T(8,128)(2,1)} %param.14), channel_id=1, source_target_pairs={{0,16},{16,32},{32,48},{48,64},{64,80},{80,96},{96,112},{112,0},{1... | collective-permute-start | bytes 3538952 | tf_op jit(solution)/shard_map/ppermute | solution.py:19
  9.0 67.6 %collective-permute-start = (s32[8]{0:T(128)}, s32[8]{0:T(128)S(1)}, u32[]{:S(2)}, u32[]{:S(2)}) collective-permute-start(s32[8]{0:T(128)} %param.17), channel_id=1, source_target_pairs={{0,16},{16,32},{32,48},{48,64},{64,80},{80,96},{96,112},{112,0},{1... | collective-permute-start | bytes 104 | tf_op jit(solution)/shard_map/ppermute | solution.py:19
  106.0 23.3 %all-to-all-start = ((bf16[16,8,2,4,512]{4,3,2,1,0:T(4,128)(2,1)}), bf16[16,8,2,4,512]{4,3,2,1,0:T(4,128)(2,1)S(1)}, u32[]{:S(2)}, u32[]{:S(2)}) async-start(bf16[16,8,2,4,512]{4,3,2,1,0:T(4,128)(2,1)} %fusion.43), calls=%async_computation | async-start | bytes 2097152 | tf_op jit(solution)/shard_map/all_to_all | solution.py:13
  114.1 154.0 %all-reduce.4.cloned.1.call-start = ((), (), s32[]{:S(2)}) async-start(), calls=%async_computation.2 | async-start | bytes 14680064 | tf_op jit(solution)/shard_map/psum | solution.py:103
  129.3 7.3 %copy-start.4 = (bf16[8,2,7168]{2,1,0:T(2,128)(2,1)S(1)}, bf16[8,2,7168]{2,1,0:T(2,128)(2,1)}, u32[]{:S(2)}) copy-start(bf16[8,2,7168]{2,1,0:T(2,128)(2,1)} %param.19) | copy-start | bytes 688132
  138.5 0.7 copy-start.8
  138.5 133.4 %copy-start.6 = (f32[7168]{0:T(1024)S(1)}, f32[7168]{0:T(1024)}, u32[]{:S(2)}) copy-start(f32[7168]{0:T(1024)} %param.22) | copy-start | bytes 86020
  138.6 198.6 %all-gather.2.cloned.1.call-start = ((), (), s32[]{:S(2)}) async-start(), calls=%async_computation.3 | async-start | bytes 8257536 | tf_op jit(solution)/shard_map/all_gather | solution.py:130
  268.1 5.2 copy-start.2
  292.0 152.2 %reduce-scatter.2.cloned.1.call-start = ((), (), s32[]{:S(2)}) async-start(), calls=%async_computation.4 | async-start | bytes 16515072 | tf_op jit(solution)/shard_map/reduce_scatter | solution.py:135
  361.6 0.7 copy-start.11
  361.6 3.9 copy-start.5
  449.9 178.5 %copy-start.1 = (bf16[4,512,128]{2,1,0:T(8,128)(2,1)S(1)}, bf16[4,512,128]{2,1,0:T(8,128)(2,1)}, u32[]{:S(2)}) copy-start(bf16[4,512,128]{2,1,0:T(8,128)(2,1)} %param.20) | copy-start | bytes 1572868
Sparse Core Ops, SparseCore 0:
  138.7 129.4 all-reduce.3
  292.2 44.9 all-gather.1
  361.7 82.5 reduce-scatter.1
